TPU v7x, 128 devices: a whole 4x4x4 slice. The times are simulated.
128 devices in a mesh: vir: 8 (over y_hi, x), occ: 16 (over y_lo, z, core).
Axes of the slice: x: 4, y: 4 (y_hi: 2, y_lo: 2; y = y_hi * 2 + y_lo), z: 4, core: 2. Of those that a mesh axis runs over, the one named last changes fastest.
Arguments:
- amplitudes: bfloat16 [4096, 8192], P('occ', 'vir'), may hold values from -6 to 6
- ladder_integrals: bfloat16 [8192, 8192], P('occ', 'vir'), may hold values from -0.0625 to 0.0625
- crossed_integrals: bfloat16 [2, 4096, 4096], P(None, 'occ', 'vir'), may hold values from -0.09375 to 0.09375
- vir_counts: int32 [8], replicated, may hold values from 1 to 64, 480 in all
Outputs:
- residual: bfloat16 [4096, 8192], P('occ', 'vir')
Inputs may be any that keep to these rules, and one draw needn't show every extreme that they name: `vir_counts`: the counts of all 8 irreps sum to 480 and the largest is exactly 64.
All inputs are finite; a program needn't handle non-finite values.
Results may differ from a plain program's by a relative error of at most 0.004.
Values may be sent and summed in bfloat16 or wider, within the bound.
A program may use at most 128 MiB of HBM per device.

v0:
```python
import jax
import jax.numpy as jnp
from jax import lax
from jax.sharding import PartitionSpec as P

O = 64
VS = 64
NB = 2
BP = 4096


def build_mask(vir_counts):
    slot_index = jnp.arange(VS, dtype=jnp.int32)
    blocks = []
    for block_index in range(NB):
        first_act = (slot_index < vir_counts[2 * block_index]).astype(jnp.float32)
        second_act = (slot_index < vir_counts[2 * block_index + 1]).astype(jnp.float32)
        blocks.append((first_act[:, None] * second_act[None, :]).reshape(BP))
    return jnp.concatenate(blocks)


def per_device(amplitudes, ladder_integrals, crossed_integrals, vir_counts):
    local_rows = amplitudes.shape[0]
    col_width = amplitudes.shape[1]
    full_mask = build_mask(vir_counts)
    column_mask = lax.dynamic_slice_in_dim(full_mask, lax.axis_index("vir") * col_width, col_width)
    masked = amplitudes * column_mask.astype(jnp.bfloat16)[None, :]
    spread = lax.all_gather(masked, "vir", axis=1, tiled=True)
    regrouped = lax.all_to_all(spread, "occ", split_axis=1, concat_axis=0, tiled=True)
    ladder = lax.psum_scatter(
        jnp.dot(regrouped, ladder_integrals, preferred_element_type=jnp.float32),
        "occ",
        scatter_dimension=0,
        tiled=True,
    )
    occ_local = local_rows // O
    reordered = (
        spread.reshape(occ_local, O, NB, VS, VS)
        .transpose(2, 0, 3, 1, 4)
        .reshape(NB, occ_local * VS, O * VS)
    )
    crossed_cols = crossed_integrals.shape[2]
    crossed_sum = jnp.einsum(
        "gxy,gyz->gxz",
        reordered,
        lax.all_gather(crossed_integrals, "occ", axis=1, tiled=True),
        preferred_element_type=jnp.float32,
    )
    crossed_term = crossed_sum.astype(jnp.bfloat16)
    occ_cols = crossed_cols // VS
    arranged = (
        crossed_term.reshape(NB, occ_local, VS, occ_cols, VS)
        .transpose(1, 3, 0, 2, 4)
        .reshape(occ_local, occ_cols, NB * VS, VS)
    )
    returned = lax.all_to_all(arranged, "vir", split_axis=2, concat_axis=1, tiled=True)
    returned = returned.reshape(local_rows, col_width)
    total = (ladder + returned.astype(jnp.float32)) * column_mask[None, :]
    return total.astype(jnp.bfloat16)


def solution(mesh):
    in_specs = (P("occ", "vir"), P("occ", "vir"), P(None, "occ", "vir"), P())
    out_specs = P("occ", "vir")
    return jax.shard_map(
        per_device, mesh=mesh, in_specs=in_specs, out_specs=out_specs, check_vma=False
    )
```

profile of v0, /device:TPU:1, one launch (start us, length us, event | category | flops | bytes accessed | tf_op | source)
XLA Modules:
  0.0 292.0 jit_solution(6605446424760793672)
XLA Ops:
  6.5 1.4 fusion.3
  8.0 1.3 compare_convert_fusion.2
  9.4 1.2 compare_convert_fusion
  10.8 1.2 copy.16
  12.0 1.0 broadcast_multiply_fusion
  13.1 0.7 all-gather.5.cloned.1.call-update
  13.9 73.4 %all-gather.3.cloned.1.call-done = bf16[256,8192]{0,1:T(8,128)(2,1)} async-done(((bf16[256,1024]{0,1:T(8,128)(2,1)}), bf16[256,8192]{0,1:T(8,128)(2,1)}) %all-gather.3.cloned.1.call-update) | async-done | bytes 4194320 | tf_op jit(solution)/shard_map/all_gather | solution.py:28
  87.2 81.4 %all_to_all.28 = bf16[256,16,512]{0,2,1:T(8,128)(2,1)} all-to-all(bf16[256,16,512]{0,2,1:T(8,128)(2,1)} %bitcast.27), channel_id=1, replica_groups=mesh['vir'=8,'occ'=16] {'occ'}, dimensions={1} | all-to-all | bytes 8388608 | tf_op jit(solution)/shard_map/all_to_all | solution.py:29
  168.7 6.4 %copy.17 = bf16[16,256,512]{2,1,0:T(8,128)(2,1)} copy(bf16[16,256,512]{1,2,0:T(8,128)(2,1)} %bitcast.28) | data formatting | bytes 8388608 | tf_op jit(solution)/shard_map/all_to_all | solution.py:29
  175.1 10.4 %fusion.4 = f32[4096,1024]{1,0:T(8,128)} fusion(bf16[4096,512]{1,0:T(8,128)(2,1)} %bitcast.30, bf16[512,1024]{1,0:T(8,128)(2,1)S(1)} %copy-done), kind=kOutput, calls=%fused_computation.15 | convolution fusion | flops 4294967296 | bytes 22020096 | tf_op jit(solution)/shard_map/dot_general | solution.py:31
  185.5 12.9 %reshape.51 = bf16[4,64,2,64,64]{1,0,4,3,2:T(4,128)(2,1)} reshape(bf16[256,8192]{0,1:T(8,128)(2,1)} %all-gather.3.cloned.1.call-done) | data formatting | bytes 8388608 | tf_op jit(solution)/shard_map/reshape | solution.py:38
  198.4 13.8 %copy.18 = bf16[4,64,2,64,64]{4,1,3,0,2:T(8,128)(2,1)} copy(bf16[4,64,2,64,64]{1,0,4,3,2:T(4,128)(2,1)} %reshape.51) | data formatting | bytes 8388608 | tf_op jit(solution)/shard_map/reshape | solution.py:38
  212.2 12.1 %reshape.52 = bf16[2,256,4096]{2,1,0:T(8,128)(2,1)} reshape(bf16[2,4,64,64,64]{4,3,2,1,0:T(8,128)(2,1)} %bitcast.26) | data formatting | bytes 8388608 | tf_op jit(solution)/shard_map/reshape | solution.py:40
  224.3 7.2 %convolution_convert_fusion = bf16[2,256,512]{2,1,0:T(8,128)(2,1)S(1)} fusion(bf16[2,256,4096]{2,1,0:T(8,128)(2,1)} %reshape.52, bf16[2,4096,512]{2,1,0:T(8,128)(2,1)} %all-gather.5.cloned.1.call-done), kind=kOutput, calls=%fused_computation.1 | convolution fusion | flops 2147745792 | bytes 13107200 | tf_op jit(solution)/shard_map/gxy,gyz->gxz/dot_general | solution.py:43
  231.5 0.5 reshape.53
  232.0 1.0 copy.19
  233.0 1.1 copy.23
  234.1 0.7 reshape.57
  234.8 12.0 %all_to_all.29 = bf16[8,2,16384]{2,1,0:T(2,128)(2,1)S(1)} all-to-all(bf16[8,2,16384]{2,1,0:T(2,128)(2,1)S(1)} %reshape.57), channel_id=1, replica_groups=mesh['vir'=8,'occ'=16] {'vir'}, dimensions={0} | all-to-all | bytes 1048576 | tf_op jit(solution)/shard_map/all_to_all | solution.py:56
  246.9 0.7 reshape.58
  247.5 0.4 copy.21
  248.5 1.5 reshape.55
  250.0 33.0 %reduce-scatter.2.cloned.1.call-done = f32[256,1024]{1,0:T(8,128)} async-done(((f32[4096,1024]{1,0:T(8,128)}), f32[256,1024]{1,0:T(8,128)}) %reduce-scatter.2.cloned.1.call-update) | async-done | bytes 1048592 | tf_op jit(solution)/shard_map/reduce_scatter | solution.py:30
  283.0 2.5 multiply_convert_fusion
  (17 shorter events, 0.9 us)
Async XLA Ops:
  6.5 168.5 %copy-start = (bf16[512,1024]{1,0:T(8,128)(2,1)S(1)}, bf16[512,1024]{1,0:T(8,128)(2,1)}, u32[]{:S(2)}) copy-start(bf16[512,1024]{1,0:T(8,128)(2,1)} %param.5) | copy-start | bytes 3145732
  6.5 80.7 %all-gather.3.cloned.1.call-start = ((), (), s32[]{:S(2)}) async-start(), calls=%async_computation.3 | async-start | bytes 4718592 | tf_op jit(solution)/shard_map/all_gather | solution.py:28
  13.1 211.2 %all-gather.5.cloned.1.call-start = ((), (), s32[]{:S(2)}) async-start(), calls=%async_computation.5 | async-start | bytes 8912896 | tf_op jit(solution)/shard_map/all_gather | solution.py:46
  13.8 269.2 %reduce-scatter.2.cloned.1.call-start = ((), (), s32[]{:S(2)}) async-start(), calls=%async_computation.4 | async-start | bytes 17825792 | tf_op jit(solution)/shard_map/reduce_scatter | solution.py:30
  247.9 37.6 %copy-start.1 = (bf16[512,1024]{1,0:T(8,128)(2,1)S(1)}, bf16[512,1024]{1,0:T(8,128)(2,1)}, u32[]{:S(2)}) copy-start(bf16[512,1024]{1,0:T(8,128)(2,1)} %param.5) | copy-start | bytes 3145732
Sparse Core Ops, SparseCore 0:
  13.2 74.0 all-gather.2
  88.9 93.0 all-gather.4
  185.6 97.3 reduce-scatter.1
where the time goes:
time: 296 us; the launch traced here: 292 us
  waiting for transfers between devices  107 us (36%)
  blocking collectives  93.5 us (32%)
  local copies, waits for them, and re-layouts  54.2 us (18%)
  matrix products  17.6 us (6%)
  between operations  13.2 us (4%)
  other arithmetic  6.43 us (2%)
    all_to_all x1, blocking collectives, per_device(): lax.all_to_all(spread, 'occ', split_axis=1, concat_axis=0, tiled=True)  81.4 us
    all_gather x1, waiting for transfers between devices, per_device(): spread = lax.all_gather(masked, 'vir', axis=1, tiled=True)  73.4 us
    reduce_scatter x1, waiting for transfers between devices, per_device(): lax.psum_scatter(jnp.dot(regrouped, ladder_integrals, preferred_element_t...  33 us
    reshape x2, local copies, waits for them, and re-layouts, per_device(): spread.reshape(occ_local, O, NB, VS, VS).transpose(2, 0, 3, 1, 4)  26.7 us
    reshape x1, local copies, waits for them, and re-layouts, per_device(): reordered = spread.reshape(occ_local, O, NB, VS, VS).transpose(2, 0, 3, 1...  12.1 us
    all_to_all x1, blocking collectives, per_device(): lax.all_to_all(arranged, 'vir', split_axis=2, concat_axis=1, tiled=True)  12 us
    dot_general x1, matrix products, per_device(): jnp.dot(regrouped, ladder_integrals, preferred_element_type=jnp.float32)  10.4 us
    dot_general x1, matrix products, per_device(): jnp.einsum('gxy,gyz->gxz', reordered, lax.all_gather(crossed_integrals, '...  7.18 us
  transfers between devices with their start and end apart: 3, of which 2 were waited for; matrix products, arithmetic and copies ran while one was open for 24% of the time, Pallas kernels for 0%

commit v1 on v0

v1 whole, which is shorter than its diff:
```python
import jax
import jax.numpy as jnp
from jax import lax
from jax.experimental import pallas as pl
from jax.experimental.pallas import tpu as pltpu
from jax.sharding import PartitionSpec as P

MESH = pl.DeviceIdType.MESH
F32 = jnp.float32
BF16 = jnp.bfloat16


def both(*conds):
    out = conds[0]
    for other in conds[1:]:
        out = jnp.logical_and(out, other)
    return out


def device(yh, x, yl, z, c):
    return (yh * 4 + x, (yl * 4 + z) * 2 + c)


def kernel(
    cnt, amp, lad, xin, out,
    mb, lb, xb, mm, rr, ff, acc, dd, pf, cs, cr, xs, xr,
    s_l, s_lf, s_m, s_mx, s_mf, s_xa, s_xd, s_xz, s_xf, s_c, s_o,
    r_m, r_l, r_x, r_c, r_o,
):
    v = lax.axis_index("vir")
    o = lax.axis_index("occ")
    yh = lax.div(v, 4)
    x = lax.rem(v, 4)
    yl = lax.div(o, 8)
    z = lax.rem(lax.div(o, 2), 4)
    c = lax.rem(o, 2)
    xp, xm = lax.rem(x + 1, 4), lax.rem(x + 3, 4)
    zp, zm, zo = lax.rem(z + 1, 4), lax.rem(z + 3, 4), lax.rem(z + 2, 4)
    q = yl * 2 + c

    def remote(src, dst, ss, rs, target):
        return pltpu.make_async_remote_copy(
            src_ref=src, dst_ref=dst, send_sem=ss, recv_sem=rs, device_id=target, device_id_type=MESH
        )

    sent = []

    def put(src, dst, ss, rs, target, cond=None, is_self=None):
        def go():
            remote(src, dst, ss, rs, target).start()

        def fin():
            remote(src, dst, ss, rs, target).wait_send()

        conds = [] if cond is None else [cond]
        if is_self is not None:
            conds.append(jnp.logical_not(is_self))

            @pl.when(both(*([] if cond is None else [cond]), is_self))
            def _():
                pltpu.make_async_copy(src, dst, rs).start()

        if conds:
            pl.when(both(*conds))(go)
            sent.append((both(*conds), fin))
        else:
            go()
            sent.append((None, fin))

    def arrived(dst, rs):
        pltpu.make_async_copy(dst, dst, rs).wait()

    def mslot(u, k):
        return mb.at[u, pl.ds(pl.multiple_of(k * 256, 256), 256)]

    def lslot(t, hf):
        return lb.at[pl.ds(pl.multiple_of((t * 2 + hf) * 256, 256), 256)]

    def xslot(k):
        return xb.at[pl.ds(pl.multiple_of(k * 256, 256), 256)]

    barrier = pltpu.get_barrier_semaphore()
    for dv in range(8):
        for dq in range(4):
            if dv == 0 and dq == 0:
                continue
            tv = lax.rem(v + dv, 8)
            tq = lax.rem(q + dq, 4)
            to = (lax.div(tq, 2) * 4 + z) * 2 + lax.rem(tq, 2)
            pl.semaphore_signal(barrier, inc=1, device_id=(tv, to), device_id_type=MESH)
    for tz in (zp, zm):
        for tc in range(2):
            pl.semaphore_signal(barrier, inc=1, device_id=device(yh, x, yl, tz, tc), device_id_type=MESH)
    pl.semaphore_wait(barrier, 35)

    ls = lax.div(z, 2)
    lt = 2 * lax.rem(z, 2) + c
    for hf, d in ((0, 0), (1, 1), (1, 0), (0, 1)):
        put(lad.at[pl.ds(hf * 256, 256)], lslot(lt, hf), s_l.at[d, hf], r_l.at[lt, hf],
            device(yh, x, yl, (zp, zm)[d], ls))
    ms = lax.div(x, 2)
    mu = lax.rem(x, 2)
    for t in range(2):
        put(amp, mslot(mu, q), s_m.at[t], r_m.at[mu, q], device(t, x, yh, z, ms),
            is_self=both(yh == t, yl == yh, c == ms))
    for hf in range(2):
        put(lad.at[pl.ds(hf * 256, 256)], lslot(lt, hf), s_l.at[2, hf], r_l.at[lt, hf],
            device(yh, x, yl, z, ls), is_self=c == ls)
    put(xin.at[1 - yl], xslot(o), s_xa, r_x.at[o], device(yh, x, 1 - yl, z, c))
    pltpu.make_async_copy(xin.at[yl], xslot(o), r_x.at[o]).start()
    put(xin.at[yl], xslot(o), s_xd.at[0], r_x.at[o], device(yh, x, yl, z, 1 - c))

    origin = c == ms
    for k in range(4):
        @pl.when(origin)
        def _():
            arrived(mslot(mu, k), r_m.at[mu, k])

        for d in range(2):
            put(mslot(mu, k), mslot(mu, k), s_mx.at[k, d], r_m.at[mu, k],
                device(yh, (xp, xm)[d], yl, z, c), cond=origin)

    for u in range(2):
        dist = lax.rem(z - (2 * c + u) + 4, 4)
        for d in range(2):
            passing = dist == (1, 3)[d]
            for tc in range(2):
                t = 2 * u + tc

                @pl.when(passing)
                def _():
                    arrived(lslot(t, d), r_l.at[t, d])

                put(lslot(t, d), lslot(t, d), s_lf.at[t, d], r_l.at[t, d],
                    device(yh, x, yl, (zp, zm)[d], c), cond=passing)

    for d in range(2):
        put(xin.at[yl], xslot(o), s_xz.at[0, d], r_x.at[o], device(yh, x, yl, (zp, zm)[d], c))
    op = ((1 - yl) * 4 + z) * 2 + c
    arrived(xslot(op), r_x.at[op])
    put(xslot(op), xslot(op), s_xd.at[1], r_x.at[op], device(yh, x, yl, z, 1 - c))
    for d in range(2):
        put(xslot(op), xslot(op), s_xz.at[1, d], r_x.at[op], device(yh, x, yl, (zp, zm)[d], c))

    for u in range(2):
        dist = lax.rem(x - (2 * c + u) + 4, 4)
        for d in range(2):
            passing = dist == (1, 3)[d]
            for k in (d, 2 + d):
                @pl.when(passing)
                def _():
                    arrived(mslot(u, k), r_m.at[u, k])

                put(mslot(u, k), mslot(u, k), s_mf.at[u, k], r_m.at[u, k],
                    device(yh, (xp, xm)[d], yl, z, c), cond=passing)

    for d in range(2):
        for b in range(2):
            k = (b * 4 + (zm, zp)[d]) * 2 + c
            arrived(xslot(k), r_x.at[k])
            if b == d:
                put(xslot(k), xslot(k), s_xf.at[d], r_x.at[k], device(yh, x, yl, (zp, zm)[d], c))
            put(xslot(k), xslot(k), s_xd.at[2 + d * 2 + b], r_x.at[k], device(yh, x, yl, z, 1 - c))
    for b in range(2):
        k = (b * 4 + zo) * 2 + c
        arrived(xslot(k), r_x.at[k])
        put(xslot(k), xslot(k), s_xd.at[6 + b], r_x.at[k], device(yh, x, yl, z, 1 - c))

    for u in range(2):
        dist = lax.rem(x - (2 * c + u) + 4, 4)
        for k in range(4):
            d = k % 2

            @pl.when(jnp.logical_and(dist != 0, dist != (1, 3)[d]))
            def _():
                arrived(mslot(u, k), r_m.at[u, k])
    for u in range(2):
        dist = lax.rem(z - (2 * c + u) + 4, 4)
        for hf in range(2):
            for tc in range(2):
                t = 2 * u + tc

                @pl.when(dist != (1, 3)[hf])
                def _():
                    arrived(lslot(t, hf), r_l.at[t, hf])

    lane = lax.broadcasted_iota(jnp.int32, (1, 1024), 1)
    slot_a = lax.div(lane, 64)
    slot_b = lax.rem(lane, 64)
    in_b = slot_b < cnt[2 * yl + 1]
    for u in range(2):
        in_a = slot_a + (32 * c + 16 * u) < cnt[2 * yl]
        mask = jnp.where(jnp.logical_and(in_a, in_b), 1.0, 0.0).astype(BF16)

        @pl.loop(0, 32)
        def _(r):
            rows = pl.ds(pl.multiple_of(r * 32, 32), 32)
            mm[rows, u * 1024:(u + 1) * 1024] = mb[u, rows, :] * mask

    for rel in (2, 1, 3, 0):
        tq = lax.rem(q + rel, 4)

        @pl.loop(0, 4)
        def _(n):
            rows = pl.ds(pl.multiple_of(tq * 256, 256), 256)
            cols = pl.ds(pl.multiple_of(n * 256, 256), 256)
            part = jnp.dot(mm[rows, :], lb[:, cols], preferred_element_type=F32)
            if rel:
                cs[rel - 1, :, cols] = part.astype(BF16)
            else:
                pf[:, cols] = part

        if rel:
            put(cs.at[rel - 1], cr.at[rel - 1], s_c.at[rel - 1], r_c.at[rel - 1],
                device(yh, x, lax.div(tq, 2), z, lax.rem(tq, 2)))

    low = lax.broadcasted_iota(jnp.int32, (16, 128), 1) < 64

    @pl.loop(0, 16)
    def _(ap):
        cols = pl.ds(pl.multiple_of(ap * 128, 128), 128)

        @pl.loop(0, 16)
        def _(r):
            rows = pl.ds(pl.multiple_of(r * 64, 64), 64)
            ff[rows, :] = mm[rows, cols].astype(F32)

        for kp in range(32):
            v0 = ff[pl.ds(2 * kp, 16, stride=64), :]
            v1 = ff[pl.ds(2 * kp + 1, 16, stride=64), :]
            turned = pltpu.roll(jnp.where(low, v1, v0), 64, 1)
            even = jnp.where(low, v0, turned)
            odd = jnp.where(low, turned, v1)
            row = pl.multiple_of(ap * 32, 32)
            rr[pl.ds(row, 32), kp * 128:(kp + 1) * 128] = jnp.concatenate([even, odd], axis=0).astype(BF16)

    arrived(xslot(o), r_x.at[o])
    for b in range(2):
        for tz in range(4):
            k = (b * 4 + tz) * 2 + 1 - c
            arrived(xslot(k), r_x.at[k])

    @pl.loop(0, 2)
    def _(m):
        for n in range(2):
            rows = pl.ds(pl.multiple_of(m * 256, 256), 256)
            acc[rows, n * 256:(n + 1) * 256] = jnp.dot(
                rr[rows, :], xb[:, n * 256:(n + 1) * 256], preferred_element_type=F32
            )

    low8 = lax.broadcasted_iota(jnp.int32, (8, 128), 1) < 64

    @pl.loop(0, 16)
    def _(ap):
        for jp in range(4):
            cols = slice(jp * 128, (jp + 1) * 128)
            for ih in range(2):
                v0 = acc[pl.ds(pl.multiple_of(ap * 32 + ih * 8, 8), 8), cols]
                v1 = acc[pl.ds(pl.multiple_of(ap * 32 + 16 + ih * 8, 8), 8), cols]
                turned = pltpu.roll(jnp.where(low8, v1, v0), 64, 1)
                dd[ap, pl.ds(ih * 64 + 2 * jp, 8, stride=8), :] = jnp.where(low8, v0, turned)
                dd[ap, pl.ds(ih * 64 + 2 * jp + 1, 8, stride=8), :] = jnp.where(low8, turned, v1)

    for u in range(2):
        for k in range(4):
            for ap in range(8):
                xs[u * 4 + k, :, ap * 128:(ap + 1) * 128] = dd[u * 8 + ap, k * 32:(k + 1) * 32, :].astype(BF16)
            put(xs.at[u * 4 + k], xr.at[v], s_o.at[u * 4 + k], r_o.at[v],
                device(yl, 2 * c + u, k // 2, z, k % 2),
                is_self=both(yh == yl, x == 2 * c + u, yl == k // 2, c == k % 2))

    for rel in range(3):
        arrived(cr.at[rel], r_c.at[rel])

    @pl.loop(0, 8)
    def _(r):
        rows = pl.ds(pl.multiple_of(r * 32, 32), 32)
        pf[rows, :] = (pf[rows, :] + cr[0, rows, :].astype(F32)) + (
            cr[1, rows, :].astype(F32) + cr[2, rows, :].astype(F32)
        )

    in_out = jnp.logical_and(slot_a + 16 * x < cnt[2 * yh], slot_b < cnt[2 * yh + 1])
    mask_out = jnp.where(in_out, 1.0, 0.0).astype(F32)
    for k in range(8):
        arrived(xr.at[k], r_o.at[k])
        got = xr[k].astype(F32)
        for i in range(4):
            rows = slice(i * 64 + k * 8, i * 64 + k * 8 + 8)
            pf[rows, :] = (pf[rows, :] + got[i * 8:(i + 1) * 8]) * mask_out

    @pl.loop(0, 8)
    def _(r):
        rows = pl.ds(pl.multiple_of(r * 32, 32), 32)
        out[rows, :] = pf[rows, :].astype(BF16)

    for cond, fin in sent:
        if cond is None:
            fin()
        else:
            pl.when(cond)(fin)


def per_device(amplitudes, ladder_integrals, crossed_integrals, vir_counts):
    dma = pltpu.SemaphoreType.DMA
    hbm = pl.BlockSpec(memory_space=pl.ANY)
    return pl.pallas_call(
        kernel,
        out_shape=jax.ShapeDtypeStruct((256, 1024), BF16),
        in_specs=[pl.BlockSpec(memory_space=pltpu.SMEM), hbm, hbm, hbm],
        out_specs=pl.BlockSpec(memory_space=pltpu.VMEM),
        scratch_shapes=[
            pltpu.VMEM((2, 1024, 1024), BF16),
            pltpu.VMEM((2048, 1024), BF16),
            pltpu.VMEM((4096, 512), BF16),
            pltpu.VMEM((1024, 2048), BF16),
            pltpu.VMEM((512, 4096), BF16),
            pltpu.VMEM((1024, 128), F32),
            pltpu.VMEM((512, 512), F32),
            pltpu.VMEM((16, 128, 128), F32),
            pltpu.VMEM((256, 1024), F32),
            pltpu.VMEM((3, 256, 1024), BF16),
            pltpu.VMEM((3, 256, 1024), BF16),
            pltpu.VMEM((8, 32, 1024), BF16),
            pltpu.VMEM((8, 32, 1024), BF16),
            dma((3, 2)), dma((4, 2)), dma((2,)), dma((4, 2)), dma((2, 4)),
            dma, dma((8,)), dma((2, 2)), dma((2,)), dma((3,)), dma((8,)),
            dma((2, 4)), dma((4, 2)), dma((16,)), dma((3,)), dma((8,)),
        ],
        compiler_params=pltpu.CompilerParams(
            collective_id=0, has_side_effects=True, vmem_limit_bytes=56 * 1024 * 1024
        ),
        name="residual",
    )(vir_counts, amplitudes, ladder_integrals, crossed_integrals)


def solution(mesh):
    in_specs = (P("occ", "vir"), P("occ", "vir"), P(None, "occ", "vir"), P())
    return jax.shard_map(
        per_device, mesh=mesh, in_specs=in_specs, out_specs=P("occ", "vir"), check_vma=False
    )
```

time: 296 us -> 105 us (0.35)
  the two profiles are of different devices: /device:TPU:1 before, /device:TPU:25 now
where the time goes in v1:
time: 105 us
  Pallas kernels  103 us (98%)
  local copies, waits for them, and re-layouts  1.87 us (2%)
    pallas_call x1, Pallas kernels, per_device(): pl.pallas_call(kernel, out_shape=jax.ShapeDtypeStruct((256, 1024), BF16),...  103 us

profile of v1, /device:TPU:25, one launch (start us, length us, event | category | flops | bytes accessed | tf_op | source)
XLA Modules:
  0.0 104.7 jit_solution(779122128036705167)
XLA Ops:
  0.0 102.8 %residual.1 = bf16[256,1024]{1,0:T(8,128)(2,1)} custom-call(s32[8]{0:T(128)} %cnt.1, bf16[256,1024]{1,0:T(8,128)(2,1)} %amp.1, bf16[512,1024]{1,0:T(8,128)(2,1)} %lad.1, bf16[2,256,512]{2,1,0:T(8,128)(2,1)} %xin.1), custom_call_target="tpu_custom_call" | custom-call | tf_op jit(solution)/shard_map/residual/pallas_call | solution.py:306
  102.8 1.9 %copy.6 = bf16[256,1024]{1,0:T(8,128)(2,1)} copy(bf16[256,1024]{1,0:T(8,128)(2,1)} %residual.1) | data formatting | bytes 1048576

commit v2 on v1

v2 whole, which is shorter than its diff:
```python
import jax
import jax.numpy as jnp
from jax import lax
from jax.experimental import pallas as pl
from jax.experimental.pallas import tpu as pltpu
from jax.sharding import PartitionSpec as P

MESH = pl.DeviceIdType.MESH
F32 = jnp.float32
BF16 = jnp.bfloat16


def both(*conds):
    out = conds[0]
    for other in conds[1:]:
        out = jnp.logical_and(out, other)
    return out


def device(yh, x, yl, z, c):
    return (yh * 4 + x, (yl * 4 + z) * 2 + c)


def rows_of(k, size):
    return pl.ds(pl.multiple_of(k * size, size), size)


def kernel(
    cnt, amp, lad, xin, out,
    mb, lb, xb, tb, mm, pp, rr, ff, acc, dd, cs, cr, xs, xr,
    s_l, s_lf, s_m, s_mt, s_mx, s_mf, s_xa, s_xd, s_xz, s_xf, s_c, s_o,
    r_m, r_t, r_l, r_x, r_c, r_o,
):
    v = lax.axis_index("vir")
    o = lax.axis_index("occ")
    yh = lax.div(v, 4)
    x = lax.rem(v, 4)
    yl = lax.div(o, 8)
    z = lax.rem(lax.div(o, 2), 4)
    c = lax.rem(o, 2)
    xn = (lax.rem(x + 1, 4), lax.rem(x + 3, 4))
    zn = (lax.rem(z + 1, 4), lax.rem(z + 3, 4))
    zo = lax.rem(z + 2, 4)
    q = yl * 2 + c
    edge = yh == yl

    def remote(src, dst, ss, rs, target):
        return pltpu.make_async_remote_copy(
            src_ref=src, dst_ref=dst, send_sem=ss, recv_sem=rs, device_id=target, device_id_type=MESH
        )

    sent = []

    def put(src, dst, ss, rs, target, cond=None, own=None):
        def go():
            remote(src, dst, ss, rs, target).start()

        def fin():
            remote(src, dst, ss, rs, target).wait_send()

        conds = [] if cond is None else [cond]
        if own is not None:
            @pl.when(both(*conds, own))
            def _():
                pltpu.make_async_copy(src, dst, rs).start()

            conds.append(jnp.logical_not(own))
        if conds:
            pl.when(both(*conds))(go)
            sent.append((both(*conds), fin))
        else:
            go()
            sent.append((None, fin))

    def arrived(dst, rs, cond=None):
        def go():
            pltpu.make_async_copy(dst, dst, rs).wait()

        if cond is None:
            go()
        else:
            pl.when(cond)(go)

    def mslot(u, k):
        return mb.at[u, rows_of(k, 256)]

    def lslot(t, hf):
        return lb.at[rows_of(t * 2 + hf, 256)]

    def xslot(k):
        return xb.at[rows_of(k, 256)]

    barrier = pltpu.get_barrier_semaphore()
    for dv in range(8):
        for dq in range(4):
            if dv == 0 and dq == 0:
                continue
            tv = lax.rem(v + dv, 8)
            tq = lax.rem(q + dq, 4)
            to = (lax.div(tq, 2) * 4 + z) * 2 + lax.rem(tq, 2)
            pl.semaphore_signal(barrier, inc=1, device_id=(tv, to), device_id_type=MESH)
    for tz in zn:
        for tc in range(2):
            pl.semaphore_signal(barrier, inc=1, device_id=device(yh, x, yl, tz, tc), device_id_type=MESH)
    pl.semaphore_wait(barrier, 35)

    ls = lax.div(z, 2)
    lt = 2 * lax.rem(z, 2) + c
    for hf, d in ((0, 0), (1, 1), (1, 0), (0, 1)):
        put(lad.at[pl.ds(hf * 256, 256)], lslot(lt, hf), s_l.at[d, hf], r_l.at[lt, hf],
            device(yh, x, yl, zn[d], ls))
    ms = lax.div(x, 2)
    mu = lax.rem(x, 2)
    put(amp, mslot(mu, q), s_m.at[0], r_m.at[mu, q], device(yh, x, yh, z, ms),
        own=both(edge, c == ms))
    put(amp, tb, s_m.at[1], r_t, device(1 - yh, x, 1 - yl, z, c), cond=edge)
    put(amp, mslot(mu, q), s_m.at[1], r_m.at[mu, q], device(1 - yh, x, yh, z, ms),
        cond=jnp.logical_not(edge))
    for hf in range(2):
        put(lad.at[pl.ds(hf * 256, 256)], lslot(lt, hf), s_l.at[2, hf], r_l.at[lt, hf],
            device(yh, x, yl, z, ls), own=c == ls)
    put(xin.at[1 - yl], xslot(o), s_xa, r_x.at[o], device(yh, x, 1 - yl, z, c))
    pltpu.make_async_copy(xin.at[yl], xslot(o), r_x.at[o]).start()
    put(xin.at[yl], xslot(o), s_xd.at[0], r_x.at[o], device(yh, x, yl, z, 1 - c))

    origin = c == ms

    def spread_amplitudes(near):
        for e in range(2):
            k = near * 2 + e
            arrived(mslot(mu, k), r_m.at[mu, k], cond=origin)
            for d in range(2):
                put(mslot(mu, k), mslot(mu, k), s_mx.at[k, d], r_m.at[mu, k],
                    device(yh, xn[d], yl, z, c), cond=origin)

    spread_amplitudes(yh)

    arrived(tb, r_t, cond=edge)
    kt = (1 - yl) * 2 + c
    put(tb, mslot(mu, kt), s_mt, r_m.at[mu, kt], device(yh, x, 1 - yh, z, ms), cond=edge)

    spread_amplitudes(1 - yh)

    for u in range(2):
        dist = lax.rem(z - (2 * c + u) + 4, 4)
        for d in range(2):
            passing = dist == (1, 3)[d]
            for t in (2 * u, 2 * u + 1):
                arrived(lslot(t, d), r_l.at[t, d], cond=passing)
                put(lslot(t, d), lslot(t, d), s_lf.at[t, d], r_l.at[t, d],
                    device(yh, x, yl, zn[d], c), cond=passing)

    for d in range(2):
        put(xin.at[yl], xslot(o), s_xz.at[0, d], r_x.at[o], device(yh, x, yl, zn[d], c))
    op = ((1 - yl) * 4 + z) * 2 + c
    arrived(xslot(op), r_x.at[op])
    for d in range(2):
        put(xslot(op), xslot(op), s_xz.at[1, d], r_x.at[op], device(yh, x, yl, zn[d], c))
    put(xslot(op), xslot(op), s_xd.at[1], r_x.at[op], device(yh, x, yl, z, 1 - c))

    for near in (yh, 1 - yh):
        for u in range(2):
            dist = lax.rem(x - (2 * c + u) + 4, 4)
            for d in range(2):
                passing = dist == (1, 3)[d]
                k = near * 2 + d
                arrived(mslot(u, k), r_m.at[u, k], cond=passing)
                put(mslot(u, k), mslot(u, k), s_mf.at[u, k], r_m.at[u, k],
                    device(yh, xn[d], yl, z, c), cond=passing)

    lane = lax.broadcasted_iota(jnp.int32, (1, 1024), 1)
    slot_a = lax.div(lane, 64)
    slot_b = lax.rem(lane, 64)
    low = lax.broadcasted_iota(jnp.int32, (16, 128), 1) < 64
    low8 = lax.broadcasted_iota(jnp.int32, (8, 128), 1) < 64

    def rest_of_amplitudes(u):
        dist = lax.rem(x - (2 * c + u) + 4, 4)
        for k in range(4):
            done = jnp.logical_or(dist == 0, dist == (1, 3)[k % 2])
            arrived(mslot(u, k), r_m.at[u, k], cond=jnp.logical_not(done))

    def rest_of_ladder(u):
        dist = lax.rem(z - (2 * c + u) + 4, 4)
        for hf in range(2):
            for t in (2 * u, 2 * u + 1):
                arrived(lslot(t, hf), r_l.at[t, hf], cond=dist != (1, 3)[hf])

    def apply_mask(u):
        act = jnp.logical_and(slot_a + (32 * c + 16 * u) < cnt[2 * yl], slot_b < cnt[2 * yl + 1])
        mask = jnp.where(act, 1.0, 0.0).astype(BF16)

        @pl.loop(0, 32)
        def _(r):
            mm[u, rows_of(r, 32), :] = mb[u, rows_of(r, 32), :] * mask

    def reorder(u):
        @pl.loop(0, 8)
        def _(ap):
            @pl.loop(0, 16)
            def _(r):
                ff[rows_of(r, 64), :] = mm[u, rows_of(r, 64), rows_of(ap, 128)].astype(F32)

            for kp in range(32):
                v0 = ff[pl.ds(2 * kp, 16, stride=64), :]
                v1 = ff[pl.ds(2 * kp + 1, 16, stride=64), :]
                turned = pltpu.roll(jnp.where(low, v1, v0), 64, 1)
                pair = jnp.concatenate([jnp.where(low, v0, turned), jnp.where(low, turned, v1)], axis=0)
                rr[rows_of(u * 8 + ap, 32), kp * 128:(kp + 1) * 128] = pair.astype(BF16)

    def ladder_first(u):
        @pl.loop(0, 16)
        def _(t):
            rows, cols = rows_of(lax.div(t, 4), 256), rows_of(lax.rem(t, 4), 256)
            pp[rows, cols] = jnp.dot(mm[u, rows, :], lb[rows_of(u, 1024), cols], preferred_element_type=F32)

    def ladder_second(u, b, slot):
        @pl.loop(0, 4)
        def _(n):
            rows, cols = rows_of(b, 256), rows_of(n, 256)
            part = pp[rows, cols] + jnp.dot(
                mm[u, rows, :], lb[rows_of(u, 1024), cols], preferred_element_type=F32
            )
            if slot is None:
                pp[rows, cols] = part
            else:
                cs[slot, :, cols] = part.astype(BF16)

    def crossed(tz, first):
        @pl.loop(0, 2)
        def _(m):
            rows = rows_of(m, 256)
            for n in range(2):
                cols = slice(n * 256, (n + 1) * 256)
                part = jnp.dot(rr[rows, rows_of(tz, 512)], xb[rows_of(tz, 512), cols], preferred_element_type=F32)
                part += jnp.dot(
                    rr[rows, rows_of(4 + tz, 512)], xb[rows_of(4 + tz, 512), cols], preferred_element_type=F32
                )
                acc[rows, cols] = part if first else acc[rows, cols] + part

    def share_crossed(k, slot):
        put(xslot(k), xslot(k), s_xd.at[slot], r_x.at[k], device(yh, x, yl, z, 1 - c))

    def pass_crossed(b, slot):
        k = (b * 4 + lax.rem(z + 3 + 2 * b, 4)) * 2 + c
        arrived(xslot(k), r_x.at[k])
        put(xslot(k), xslot(k), s_xf.at[slot], r_x.at[k],
            device(yh, x, yl, lax.rem(z + 1 + 2 * b, 4), c))
        share_crossed(k, 2 + slot)

    u0 = jnp.where(origin, mu, 1 - mu)
    u1 = 1 - u0
    rest_of_amplitudes(u0)
    apply_mask(u0)
    reorder(u0)
    rest_of_ladder(u0)
    ladder_first(u0)
    pass_crossed(yl, 0)
    rest_of_amplitudes(u1)
    apply_mask(u1)
    rest_of_ladder(u1)

    ladder_second(u1, (1 - yl) * 2 + 1 - c, 0)
    put(cs.at[0], cr.at[0], s_c.at[0], r_c.at[0], device(yh, x, yl, z, 1 - c))
    ladder_second(u1, yl * 2 + 1 - c, 1)
    put(cs.at[1], cr.at[1], s_c.at[1], r_c.at[1], device(yh, x, yl, z, 1 - c))
    ladder_second(u1, (1 - yl) * 2 + c, None)
    arrived(cr.at[0], r_c.at[0])

    @pl.loop(0, 8)
    def _(r):
        part = pp[rows_of(((1 - yl) * 2 + c) * 8 + r, 32), :] + cr[0, rows_of(r, 32), :].astype(F32)
        cs[2, rows_of(r, 32), :] = part.astype(BF16)

    put(cs.at[2], cr.at[2], s_c.at[2], r_c.at[2], device(yh, x, 1 - yl, z, c))
    ladder_second(u1, q, None)
    pass_crossed(1 - yl, 1)
    reorder(u1)

    for d in range(2):
        k = ((1 - d) * 4 + zn[1 - d]) * 2 + c
        arrived(xslot(k), r_x.at[k])
        share_crossed(k, 4 + d)
    arrived(xslot(o), r_x.at[o])

    def other_core(tz):
        for b in range(2):
            k = (b * 4 + tz) * 2 + 1 - c
            arrived(xslot(k), r_x.at[k])

    other_core(z)
    crossed(z, True)
    for b in range(2):
        k = (b * 4 + zo) * 2 + c
        arrived(xslot(k), r_x.at[k])
        share_crossed(k, 6 + b)
    for tz in (zn[0], zn[1], zo):
        other_core(tz)
        crossed(tz, False)

    def back():
        @pl.loop(0, 16)
        def _(ap):
            for jp in range(4):
                cols = slice(jp * 128, (jp + 1) * 128)
                for ih in range(2):
                    v0 = acc[rows_of(ap * 4 + ih, 8), cols]
                    v1 = acc[rows_of(ap * 4 + 2 + ih, 8), cols]
                    turned = pltpu.roll(jnp.where(low8, v1, v0), 64, 1)
                    dd[ap, pl.ds(ih * 64 + 2 * jp, 8, stride=8), :] = jnp.where(low8, v0, turned)
                    dd[ap, pl.ds(ih * 64 + 2 * jp + 1, 8, stride=8), :] = jnp.where(low8, turned, v1)

    back()
    for u in range(2):
        for k in range(4):
            for ap in range(8):
                xs[u * 4 + k, :, ap * 128:(ap + 1) * 128] = dd[u * 8 + ap, k * 32:(k + 1) * 32, :].astype(BF16)
            put(xs.at[u * 4 + k], xr.at[v], s_o.at[u * 4 + k], r_o.at[v],
                device(yl, 2 * c + u, k // 2, z, k % 2),
                own=both(yh == yl, x == 2 * c + u, yl == k // 2, c == k % 2))

    arrived(cr.at[1], r_c.at[1])
    arrived(cr.at[2], r_c.at[2])

    @pl.loop(0, 8)
    def _(r):
        rows = rows_of(q * 8 + r, 32)
        pp[rows, :] = pp[rows, :] + (cr[1, rows_of(r, 32), :].astype(F32) + cr[2, rows_of(r, 32), :].astype(F32))

    act_out = jnp.logical_and(slot_a + 16 * x < cnt[2 * yh], slot_b < cnt[2 * yh + 1])
    mask_out = jnp.where(act_out, 1.0, 0.0).astype(F32)
    for k in range(8):
        arrived(xr.at[k], r_o.at[k])
        got = xr[k].astype(F32)
        for i in range(4):
            rows = rows_of(q * 32 + i * 8 + k, 8)
            pp[rows, :] = (pp[rows, :] + got[i * 8:(i + 1) * 8]) * mask_out

    @pl.loop(0, 8)
    def _(r):
        out[rows_of(r, 32), :] = pp[rows_of(q * 8 + r, 32), :].astype(BF16)

    for cond, fin in sent:
        if cond is None:
            fin()
        else:
            pl.when(cond)(fin)


def per_device(amplitudes, ladder_integrals, crossed_integrals, vir_counts):
    dma = pltpu.SemaphoreType.DMA
    hbm = pl.BlockSpec(memory_space=pl.ANY)
    return pl.pallas_call(
        kernel,
        out_shape=jax.ShapeDtypeStruct((256, 1024), BF16),
        in_specs=[pl.BlockSpec(memory_space=pltpu.SMEM), hbm, hbm, hbm],
        out_specs=pl.BlockSpec(memory_space=pltpu.VMEM),
        scratch_shapes=[
            pltpu.VMEM((2, 1024, 1024), BF16),
            pltpu.VMEM((2048, 1024), BF16),
            pltpu.VMEM((4096, 512), BF16),
            pltpu.VMEM((256, 1024), BF16),
            pltpu.VMEM((2, 1024, 1024), BF16),
            pltpu.VMEM((1024, 1024), F32),
            pltpu.VMEM((512, 4096), BF16),
            pltpu.VMEM((1024, 128), F32),
            pltpu.VMEM((512, 512), F32),
            pltpu.VMEM((16, 128, 128), F32),
            pltpu.VMEM((3, 256, 1024), BF16),
            pltpu.VMEM((3, 256, 1024), BF16),
            pltpu.VMEM((8, 32, 1024), BF16),
            pltpu.VMEM((8, 32, 1024), BF16),
            dma((3, 2)), dma((4, 2)), dma((2,)), dma, dma((4, 2)), dma((2, 4)),
            dma, dma((8,)), dma((2, 2)), dma((2,)), dma((3,)), dma((8,)),
            dma((2, 4)), dma, dma((4, 2)), dma((16,)), dma((3,)), dma((8,)),
        ],
        compiler_params=pltpu.CompilerParams(
            collective_id=0, has_side_effects=True, vmem_limit_bytes=56 * 1024 * 1024
        ),
        name="residual",
    )(vir_counts, amplitudes, ladder_integrals, crossed_integrals)


def solution(mesh):
    in_specs = (P("occ", "vir"), P("occ", "vir"), P(None, "occ", "vir"), P())
    return jax.shard_map(
        per_device, mesh=mesh, in_specs=in_specs, out_specs=P("occ", "vir"), check_vma=False
    )
```

time: 105 us -> 95 us (0.905)
  the two profiles are of different devices: /device:TPU:25 before, /device:TPU:1 now
where the time goes in v2:
time: 95 us; the launch traced here: 93.9 us
  Pallas kernels  92 us (97%)
  local copies, waits for them, and re-layouts  1.87 us (2%)
    pallas_call x1, Pallas kernels, per_device(): pl.pallas_call(kernel, out_shape=jax.ShapeDtypeStruct((256, 1024), BF16),...  92 us

profile of v2, /device:TPU:1, one launch (start us, length us, event | category | flops | bytes accessed | tf_op | source)
XLA Modules:
  0.0 93.9 jit_solution(5431676678535823631)
XLA Ops:
  0.0 92.0 %residual.1 = bf16[256,1024]{1,0:T(8,128)(2,1)} custom-call(s32[8]{0:T(128)} %cnt.1, bf16[256,1024]{1,0:T(8,128)(2,1)} %amp.1, bf16[512,1024]{1,0:T(8,128)(2,1)} %lad.1, bf16[2,256,512]{2,1,0:T(8,128)(2,1)} %xin.1), custom_call_target="tpu_custom_call" | custom-call | tf_op jit(solution)/shard_map/residual/pallas_call | solution.py:353
  92.0 1.9 %copy.6 = bf16[256,1024]{1,0:T(8,128)(2,1)} copy(bf16[256,1024]{1,0:T(8,128)(2,1)} %residual.1) | data formatting | bytes 1048576

commit v3 on v2

v3 whole, which is shorter than its diff:
```python
import jax
import jax.numpy as jnp
from jax import lax
from jax.experimental import pallas as pl
from jax.experimental.pallas import tpu as pltpu
from jax.sharding import PartitionSpec as P

MESH = pl.DeviceIdType.MESH
F32 = jnp.float32
BF16 = jnp.bfloat16
NP = 4


def both(*conds):
    out = conds[0]
    for other in conds[1:]:
        out = jnp.logical_and(out, other)
    return out


def device(yh, x, yl, z, c):
    return (yh * 4 + x, (yl * 4 + z) * 2 + c)


def rows_of(k, size):
    return pl.ds(pl.multiple_of(k * size, size), size)


def kernel(
    cnt, amp, lad, xin, out,
    mb, lb, xb, tb, mm, pp, rr, ff, acc, dd, cs, cr, xs, xr,
    s_l, s_lf, s_m, s_mt, s_mx, s_mf, s_xa, s_xd, s_xz, s_xf, s_c, s_o,
    r_m, r_t, r_l, r_x, r_c, r_o,
):
    v = lax.axis_index("vir")
    o = lax.axis_index("occ")
    yh = lax.div(v, 4)
    x = lax.rem(v, 4)
    yl = lax.div(o, 8)
    z = lax.rem(lax.div(o, 2), 4)
    c = lax.rem(o, 2)
    xn = (lax.rem(x + 1, 4), lax.rem(x + 3, 4))
    zn = (lax.rem(z + 1, 4), lax.rem(z + 3, 4))
    zo = lax.rem(z + 2, 4)
    q = yl * 2 + c
    edge = yh == yl
    inner = jnp.logical_not(edge)

    def put(src, dst, ss, rs, target, cond=None, own=None):
        def go():
            pltpu.make_async_remote_copy(
                src_ref=src, dst_ref=dst, send_sem=ss, recv_sem=rs, device_id=target, device_id_type=MESH
            ).start()

        if own is not None:
            @pl.when(own)
            def _():
                pltpu.make_async_copy(src, dst, rs).start()

            cond = jnp.logical_not(own)
        if cond is None:
            go()
        else:
            pl.when(cond)(go)

    def arrived(ref, sem, cond=None):
        def go():
            pltpu.make_async_copy(ref, ref, sem).wait()

        if cond is None:
            go()
        else:
            pl.when(cond)(go)

    PR = 256 // NP

    def mslot(u, k, p):
        return mb.at[u, rows_of(k * NP + p, PR)]

    def lslot(t, hf):
        return lb.at[rows_of(t * 2 + hf, 256)]

    def xslot(h, k):
        return xb.at[h, rows_of(k, 256)]

    def xpart(g, h):
        return xin.at[g, :, pl.ds(h * 256, 256)]

    barrier = pltpu.get_barrier_semaphore()
    for dv in range(8):
        for dq in range(4):
            if dv == 0 and dq == 0:
                continue
            tv = lax.rem(v + dv, 8)
            tq = lax.rem(q + dq, 4)
            to = (lax.div(tq, 2) * 4 + z) * 2 + lax.rem(tq, 2)
            pl.semaphore_signal(barrier, inc=1, device_id=(tv, to), device_id_type=MESH)
    for tz in zn:
        for tc in range(2):
            pl.semaphore_signal(barrier, inc=1, device_id=device(yh, x, yl, tz, tc), device_id_type=MESH)
    pl.semaphore_wait(barrier, 35)

    ls = lax.div(z, 2)
    lt = 2 * lax.rem(z, 2) + c
    for hf, d in ((0, 0), (1, 1), (1, 0), (0, 1)):
        put(lad.at[pl.ds(hf * 256, 256)], lslot(lt, hf), s_l.at[d], r_l.at[lt, hf],
            device(yh, x, yl, zn[d], ls))
    ms = lax.div(x, 2)
    mu = lax.rem(x, 2)
    for p in range(NP):
        part = amp.at[pl.ds(p * PR, PR)]
        put(part, mslot(mu, q, p), s_m.at[0], r_m.at[mu, q, p], device(yh, x, yh, z, ms),
            own=both(edge, c == ms))
        put(part, tb.at[pl.ds(p * PR, PR)], s_m.at[1], r_t.at[p], device(1 - yh, x, 1 - yl, z, c),
            cond=edge)
        put(part, mslot(mu, q, p), s_m.at[1], r_m.at[mu, q, p], device(1 - yh, x, yh, z, ms),
            cond=inner)
    for h in range(2):
        put(xpart(1 - yl, h), xslot(h, o), s_xa, r_x.at[h, o], device(yh, x, 1 - yl, z, c))
    for hf in range(2):
        put(lad.at[pl.ds(hf * 256, 256)], lslot(lt, hf), s_l.at[2], r_l.at[lt, hf],
            device(yh, x, yl, z, ls), own=c == ls)
    for h in range(2):
        pltpu.make_async_copy(xpart(yl, h), xslot(h, o), r_x.at[h, o]).start()
        put(xpart(yl, h), xslot(h, o), s_xd.at[h], r_x.at[h, o], device(yh, x, yl, z, 1 - c))

    origin = c == ms

    def spread_amplitudes(k, p):
        arrived(mslot(mu, k, p), r_m.at[mu, k, p], cond=origin)
        for d in range(2):
            put(mslot(mu, k, p), mslot(mu, k, p), s_mx.at[d], r_m.at[mu, k, p],
                device(yh, xn[d], yl, z, c), cond=origin)

    for p in range(NP):
        for e in range(2):
            spread_amplitudes(yh * 2 + e, p)
    kt = (1 - yl) * 2 + c
    for p in range(NP):
        part = tb.at[pl.ds(p * PR, PR)]
        arrived(part, r_t.at[p], cond=edge)
        put(part, mslot(mu, kt, p), s_mt, r_m.at[mu, kt, p], device(yh, x, 1 - yh, z, ms), cond=edge)
        for e in range(2):
            spread_amplitudes((1 - yh) * 2 + e, p)

    ldist = [lax.rem(z - (2 * c + u) + 4, 4) for u in range(2)]
    for u in range(2):
        for d in range(2):
            passing = ldist[u] == (1, 3)[d]
            for t in (2 * u, 2 * u + 1):
                arrived(lslot(t, d), r_l.at[t, d], cond=passing)
                put(lslot(t, d), lslot(t, d), s_lf, r_l.at[t, d],
                    device(yh, x, yl, zn[d], c), cond=passing)

    op = ((1 - yl) * 4 + z) * 2 + c

    def send_own(h):
        for d in range(2):
            put(xpart(yl, h), xslot(h, o), s_xz.at[h, d], r_x.at[h, o], device(yh, x, yl, zn[d], c))

    def share_crossed(h, k):
        put(xslot(h, k), xslot(h, k), s_xd.at[h], r_x.at[h, k], device(yh, x, yl, z, 1 - c))

    def send_other(h):
        arrived(xslot(h, op), r_x.at[h, op])
        for d in range(2):
            put(xslot(h, op), xslot(h, op), s_xz.at[h, d], r_x.at[h, op], device(yh, x, yl, zn[d], c))
        share_crossed(h, op)

    def pass_crossed(h, b):
        k = (b * 4 + lax.rem(z + 3 + 2 * b, 4)) * 2 + c
        arrived(xslot(h, k), r_x.at[h, k])
        put(xslot(h, k), xslot(h, k), s_xf.at[h], r_x.at[h, k],
            device(yh, x, yl, lax.rem(z + 1 + 2 * b, 4), c))
        share_crossed(h, k)

    def take_near(h):
        for d in range(2):
            k = ((1 - d) * 4 + zn[1 - d]) * 2 + c
            arrived(xslot(h, k), r_x.at[h, k])
            share_crossed(h, k)

    def take_far(h):
        for b in range(2):
            k = (b * 4 + zo) * 2 + c
            arrived(xslot(h, k), r_x.at[h, k])
            share_crossed(h, k)

    def other_core(h, tz):
        for b in range(2):
            k = (b * 4 + tz) * 2 + 1 - c
            arrived(xslot(h, k), r_x.at[h, k])

    send_own(0)
    send_other(0)
    send_own(1)

    lane = lax.broadcasted_iota(jnp.int32, (1, 1024), 1)
    slot_a = lax.div(lane, 64)
    slot_b = lax.rem(lane, 64)
    low = lax.broadcasted_iota(jnp.int32, (16, 128), 1) < 64
    low8 = lax.broadcasted_iota(jnp.int32, (8, 128), 1) < 64

    def rest_of_amplitudes(u):
        dist = lax.rem(x - (2 * c + u) + 4, 4)
        for k in range(4):
            done = jnp.logical_or(dist == 0, dist == (1, 3)[k % 2])
            for p in range(NP):
                arrived(mslot(u, k, p), r_m.at[u, k, p], cond=jnp.logical_not(done))

    def rest_of_ladder(u):
        dist = lax.rem(z - (2 * c + u) + 4, 4)
        for hf in range(2):
            for t in (2 * u, 2 * u + 1):
                arrived(lslot(t, hf), r_l.at[t, hf], cond=dist != (1, 3)[hf])

    def apply_mask(u):
        act = jnp.logical_and(slot_a + (32 * c + 16 * u) < cnt[2 * yl], slot_b < cnt[2 * yl + 1])
        mask = jnp.where(act, 1.0, 0.0).astype(BF16)

        @pl.loop(0, 32)
        def _(r):
            mm[u, rows_of(r, 32), :] = mb[u, rows_of(r, 32), :] * mask

    def reorder(u):
        @pl.loop(0, 8)
        def _(ap):
            @pl.loop(0, 16)
            def _(r):
                ff[pl.ds(pl.multiple_of(r * 72, 8), 64), :] = mm[u, rows_of(r, 64), rows_of(ap, 128)].astype(F32)

            for kp in range(32):
                v0 = ff[pl.ds(2 * kp, 16, stride=72), :]
                v1 = ff[pl.ds(2 * kp + 1, 16, stride=72), :]
                turned = pltpu.roll(jnp.where(low, v1, v0), 64, 1)
                pair = jnp.concatenate([jnp.where(low, v0, turned), jnp.where(low, turned, v1)], axis=0)
                rr[rows_of(u * 8 + ap, 32), kp * 128:(kp + 1) * 128] = pair.astype(BF16)

    def ladder_first(u):
        @pl.loop(0, 16)
        def _(t):
            rows, cols = rows_of(lax.div(t, 4), 256), rows_of(lax.rem(t, 4), 256)
            pp[rows, cols] = jnp.dot(mm[u, rows, :], lb[rows_of(u, 1024), cols], preferred_element_type=F32)

    def ladder_second(u, b, slot):
        @pl.loop(0, 4)
        def _(n):
            rows, cols = rows_of(b, 256), rows_of(n, 256)
            part = pp[rows, cols] + jnp.dot(
                mm[u, rows, :], lb[rows_of(u, 1024), cols], preferred_element_type=F32
            )
            if slot is None:
                pp[rows, cols] = part
            else:
                cs[slot, :, cols] = part.astype(BF16)

    def crossed(h, tz, first):
        @pl.loop(0, 2)
        def _(m):
            rows = rows_of(m, 256)
            part = jnp.dot(rr[rows, rows_of(tz, 512)], xb[h, rows_of(tz, 512), :], preferred_element_type=F32)
            part += jnp.dot(
                rr[rows, rows_of(4 + tz, 512)], xb[h, rows_of(4 + tz, 512), :], preferred_element_type=F32
            )
            acc[rows, :] = part if first else acc[rows, :] + part

    def back(u):
        @pl.loop(0, 8)
        def _(ap):
            for jp in range(2):
                cols = slice(jp * 128, (jp + 1) * 128)
                for ih in range(2):
                    v0 = acc[rows_of((u * 8 + ap) * 4 + ih, 8), cols]
                    v1 = acc[rows_of((u * 8 + ap) * 4 + 2 + ih, 8), cols]
                    turned = pltpu.roll(jnp.where(low8, v1, v0), 64, 1)
                    dd[ap, pl.ds(ih * 32 + 2 * jp, 8, stride=4), :] = jnp.where(low8, v0, turned)
                    dd[ap, pl.ds(ih * 32 + 2 * jp + 1, 8, stride=4), :] = jnp.where(low8, turned, v1)

    own_out = both(edge, origin)

    def give_back(h):
        for u in range(2):
            back(u)
            for k in range(4):
                for ap in range(8):
                    xs[h, u * 4 + k, :, ap * 128:(ap + 1) * 128] = dd[ap, k * 16:(k + 1) * 16, :].astype(BF16)
                put(xs.at[h, u * 4 + k], xr.at[h, v], s_o.at[h], r_o.at[h, v],
                    device(yl, 2 * c + u, k // 2, z, k % 2),
                    own=both(own_out, mu == u, q == k))

    u0 = jnp.where(origin, mu, 1 - mu)
    u1 = 1 - u0

    def prepare(u):
        apply_mask(u)
        reorder(u)

    @pl.when(origin)
    def _():
        prepare(u0)

    for near in (yh, 1 - yh):
        for p in range(NP):
            for u in range(2):
                dist = lax.rem(x - (2 * c + u) + 4, 4)
                for d in range(2):
                    passing = dist == (1, 3)[d]
                    k = near * 2 + d
                    arrived(mslot(u, k, p), r_m.at[u, k, p], cond=passing)
                    put(mslot(u, k, p), mslot(u, k, p), s_mf, r_m.at[u, k, p],
                        device(yh, xn[d], yl, z, c), cond=passing)

    @pl.when(jnp.logical_not(origin))
    def _():
        rest_of_amplitudes(u0)
        prepare(u0)

    rest_of_ladder(u0)
    ladder_first(u0)
    pass_crossed(0, yl)
    rest_of_amplitudes(u1)
    apply_mask(u1)
    rest_of_ladder(u1)

    ladder_second(u1, (1 - yl) * 2 + 1 - c, 0)
    put(cs.at[0], cr.at[0], s_c.at[0], r_c.at[0], device(yh, x, yl, z, 1 - c))
    ladder_second(u1, yl * 2 + 1 - c, 1)
    put(cs.at[1], cr.at[1], s_c.at[1], r_c.at[1], device(yh, x, yl, z, 1 - c))
    pass_crossed(0, 1 - yl)
    send_other(1)
    ladder_second(u1, (1 - yl) * 2 + c, None)
    arrived(cr.at[0], r_c.at[0])

    @pl.loop(0, 8)
    def _(r):
        part = pp[rows_of(((1 - yl) * 2 + c) * 8 + r, 32), :] + cr[0, rows_of(r, 32), :].astype(F32)
        cs[2, rows_of(r, 32), :] = part.astype(BF16)

    put(cs.at[2], cr.at[2], s_c.at[2], r_c.at[2], device(yh, x, 1 - yl, z, c))
    ladder_second(u1, q, None)
    pass_crossed(1, yl)
    take_near(0)
    reorder(u1)
    pass_crossed(1, 1 - yl)
    take_far(0)

    for h in range(2):
        arrived(xslot(h, o), r_x.at[h, o])
        for tz in (z, zn[0], zn[1], zo):
            if h == 1 and tz is zn[0]:
                take_near(1)
            if h == 1 and tz is zo:
                take_far(1)
            other_core(h, tz)
            crossed(h, tz, tz is z)
        give_back(h)

    arrived(cr.at[1], r_c.at[1])
    arrived(cr.at[2], r_c.at[2])
    act_out = jnp.logical_and(slot_a + 16 * x < cnt[2 * yh], slot_b < cnt[2 * yh + 1])
    mask_out = jnp.where(act_out, 1.0, 0.0).astype(F32)

    @pl.loop(0, 8)
    def _(r):
        rows = rows_of(q * 8 + r, 32)
        pp[rows, :] = pp[rows, :] + (cr[1, rows_of(r, 32), :].astype(F32) + cr[2, rows_of(r, 32), :].astype(F32))

    for d in range(3):
        arrived(lad, s_l.at[d], cond=None if d < 2 else c != ls)
    lpass = [jnp.logical_or(ldist[u] == 1, ldist[u] == 3) for u in range(2)]
    for u in range(2):
        arrived(lb.at[pl.ds(0, 512)], s_lf, cond=lpass[u])
    arrived(amp, s_m.at[0], cond=jnp.logical_not(own_out))
    arrived(amp, s_m.at[1])
    arrived(tb, s_mt, cond=edge)
    for d in range(2):
        arrived(mb.at[0], s_mx.at[d], cond=origin)
    arrived(mb.at[0, pl.ds(0, 512)], s_mf)
    arrived(xb.at[pl.ds(0, 2), pl.ds(0, 256)], s_xa)
    for h in range(2):
        arrived(xb.at[h, pl.ds(0, 2048)], s_xd.at[h])
        arrived(xb.at[h, pl.ds(0, 512)], s_xf.at[h])
        for d in range(2):
            arrived(xb.at[h, pl.ds(0, 512)], s_xz.at[h, d])
    for k in range(3):
        arrived(cs.at[k], s_c.at[k])

    for kk in range(4):
        got = []
        for k in (2 * kk, 2 * kk + 1):
            for h in range(2):
                arrived(xr.at[h, k], r_o.at[h, k])
            got.append([xr[h, k].astype(F32) for h in range(2)])
        for i in range(4):
            part = jnp.concatenate([g[h][i * 4:i * 4 + 4] for g in got for h in range(2)], axis=0)
            rows = rows_of(q * 16 + i * 4 + kk, 16)
            out[i * 64 + kk * 16:i * 64 + kk * 16 + 16, :] = ((pp[rows, :] + part) * mask_out).astype(BF16)

    for h in range(2):
        arrived(xs.at[h], s_o.at[h], cond=jnp.logical_not(own_out))
        arrived(xs.at[h, pl.ds(0, 7)], s_o.at[h], cond=own_out)


def per_device(amplitudes, ladder_integrals, crossed_integrals, vir_counts):
    dma = pltpu.SemaphoreType.DMA
    hbm = pl.BlockSpec(memory_space=pl.ANY)
    return pl.pallas_call(
        kernel,
        out_shape=pltpu.VMEM((256, 1024), BF16),
        in_specs=[pl.BlockSpec(memory_space=pltpu.SMEM), hbm, hbm, hbm],
        out_specs=pl.BlockSpec(memory_space=pltpu.VMEM),
        scratch_shapes=[
            pltpu.VMEM((2, 1024, 1024), BF16),
            pltpu.VMEM((2048, 1024), BF16),
            pltpu.VMEM((2, 4096, 256), BF16),
            pltpu.VMEM((256, 1024), BF16),
            pltpu.VMEM((2, 1024, 1024), BF16),
            pltpu.VMEM((1024, 1024), F32),
            pltpu.VMEM((512, 4096), BF16),
            pltpu.VMEM((1152, 128), F32),
            pltpu.VMEM((512, 256), F32),
            pltpu.VMEM((8, 64, 128), F32),
            pltpu.VMEM((3, 256, 1024), BF16),
            pltpu.VMEM((3, 256, 1024), BF16),
            pltpu.VMEM((2, 8, 16, 1024), BF16),
            pltpu.VMEM((2, 8, 16, 1024), BF16),
            dma((3,)), dma, dma((2,)), dma, dma((2,)), dma,
            dma, dma((2,)), dma((2, 2)), dma((2,)), dma((3,)), dma((2,)),
            dma((2, 4, NP)), dma((NP,)), dma((4, 2)), dma((2, 16)), dma((3,)), dma((2, 8)),
        ],
        compiler_params=pltpu.CompilerParams(
            collective_id=0, has_side_effects=True, vmem_limit_bytes=56 * 1024 * 1024
        ),
        name="residual",
    )(vir_counts, amplitudes, ladder_integrals, crossed_integrals)


def solution(mesh):
    in_specs = (P("occ", "vir"), P("occ", "vir"), P(None, "occ", "vir"), P())
    return jax.shard_map(
        per_device, mesh=mesh, in_specs=in_specs, out_specs=P("occ", "vir"), check_vma=False
    )
```

time: 95 us -> 81.6 us (0.86); the launches traced: 93.9 us -> 81.5 us
  Pallas kernels: 92 us -> 80.7 us
  local copies, waits for them, and re-layouts: 1.87 us -> 0.8 us
    pallas_call x1, Pallas kernels: 92 us -> 80.7 us  [per_device(): pl.pallas_call(kernel, out_shape=pltpu.VMEM((256, 1024), BF16), in_specs=...]
    unnamed x1, local copies, waits for them, and re-layouts: 1.87 us -> 0.8 us
where the time goes in v3:
time: 81.6 us; the launch traced here: 81.5 us
  Pallas kernels  80.7 us (99%)
    pallas_call x1, Pallas kernels, per_device(): pl.pallas_call(kernel, out_shape=pltpu.VMEM((256, 1024), BF16), in_specs=...  80.7 us

profile of v3, /device:TPU:1, one launch (start us, length us, event | category | flops | bytes accessed | tf_op | source)
XLA Modules:
  0.0 81.5 jit_solution(10959025955137089281)
XLA Ops:
  0.0 80.7 %residual.1 = bf16[256,1024]{1,0:T(8,128)(2,1)S(1)} custom-call(s32[8]{0:T(128)} %cnt.1, bf16[256,1024]{1,0:T(8,128)(2,1)} %amp.1, bf16[512,1024]{1,0:T(8,128)(2,1)} %lad.1, bf16[2,256,512]{2,1,0:T(8,128)(2,1)} %xin.1), custom_call_target="tpu_custom_call" | custom-call | tf_op jit(solution)/shard_map/residual/pallas_call | solution.py:407
  80.7 0.8 copy.6

commit v4 on v3

v4 whole, which is shorter than its diff:
```python
import jax
import jax.numpy as jnp
from jax import lax
from jax.experimental import pallas as pl
from jax.experimental.pallas import tpu as pltpu
from jax.sharding import PartitionSpec as P

MESH = pl.DeviceIdType.MESH
F32 = jnp.float32
BF16 = jnp.bfloat16
NP = 4


def both(*conds):
    out = conds[0]
    for other in conds[1:]:
        out = jnp.logical_and(out, other)
    return out


def device(yh, x, yl, z, c):
    return (yh * 4 + x, (yl * 4 + z) * 2 + c)


def rows_of(k, size):
    return pl.ds(pl.multiple_of(k * size, size), size)


def kernel(
    cnt, amp, lad, xin, out,
    mb, lb, xb, tb, xt, tt, mm, pp, rr, ff, acc, dd, cs, cr, xs, xr,
    s_l, s_lf, s_m, s_mt, s_mx, s_mf, s_t, s_tf, s_y, s_xa, s_xd, s_xz, s_xf, s_c, s_o,
    r_m, r_t, r_xt, r_tt, r_l, r_lf, r_x, r_c, r_o,
):
    v = lax.axis_index("vir")
    o = lax.axis_index("occ")
    yh = lax.div(v, 4)
    x = lax.rem(v, 4)
    yl = lax.div(o, 8)
    z = lax.rem(lax.div(o, 2), 4)
    c = lax.rem(o, 2)
    xn = (lax.rem(x + 1, 4), lax.rem(x + 3, 4))
    zn = (lax.rem(z + 1, 4), lax.rem(z + 3, 4))
    zo = lax.rem(z + 2, 4)
    q = yl * 2 + c
    edge = yh == yl
    inner = jnp.logical_not(edge)

    def put(src, dst, ss, rs, target, cond=None, own=None):
        def go():
            pltpu.make_async_remote_copy(
                src_ref=src, dst_ref=dst, send_sem=ss, recv_sem=rs, device_id=target, device_id_type=MESH
            ).start()

        if own is not None:
            @pl.when(own)
            def _():
                pltpu.make_async_copy(src, dst, rs).start()

            cond = jnp.logical_not(own)
        if cond is None:
            go()
        else:
            pl.when(cond)(go)

    def arrived(ref, sem, cond=None):
        def go():
            pltpu.make_async_copy(ref, ref, sem).wait()

        if cond is None:
            go()
        else:
            pl.when(cond)(go)

    PR = 256 // NP

    def mslot(u, k, p):
        return mb.at[u, rows_of(k * NP + p, PR)]

    def lslot(t, hf):
        return lb.at[rows_of(t * 2 + hf, 256)]

    def xslot(k):
        return xb.at[rows_of(k, 256)]

    barrier = pltpu.get_barrier_semaphore()
    for dv in range(8):
        for dq in range(4):
            if dv == 0 and dq == 0:
                continue
            tv = lax.rem(v + dv, 8)
            tq = lax.rem(q + dq, 4)
            to = (lax.div(tq, 2) * 4 + z) * 2 + lax.rem(tq, 2)
            pl.semaphore_signal(barrier, inc=1, device_id=(tv, to), device_id_type=MESH)
    for tz in zn:
        for tc in range(2):
            pl.semaphore_signal(barrier, inc=1, device_id=device(yh, x, yl, tz, tc), device_id_type=MESH)
    pl.semaphore_wait(barrier, 35)

    put(xin.at[1 - yl], xslot(o), s_xa, r_x.at[o], device(yh, x, 1 - yl, z, c))
    for d in range(2):
        put(xin.at[yl], xslot(o), s_xz.at[d], r_x.at[o], device(yh, x, yl, zn[d], c))
    ms = lax.div(x, 2)
    mu = lax.rem(x, 2)
    LP = NP - 1
    for d in range(2):
        put(amp.at[pl.ds(LP * PR, PR)], xt.at[d], s_t.at[d], r_xt.at[d], device(yh, xn[d], yl, z, c))
    for p in range(NP):
        part = amp.at[pl.ds(p * PR, PR)]
        put(part, mslot(mu, q, p), s_m.at[0], r_m.at[mu, q, p], device(yh, x, yh, z, ms),
            own=both(edge, c == ms))
        put(part, tb.at[pl.ds(p * PR, PR)], s_m.at[1], r_t.at[p], device(1 - yh, x, 1 - yl, z, c),
            cond=edge)
        put(part, mslot(mu, q, p), s_m.at[1], r_m.at[mu, q, p], device(1 - yh, x, yh, z, ms),
            cond=inner)
    pltpu.make_async_copy(xin.at[yl], xslot(o), r_x.at[o]).start()

    def share_crossed(k, src=None):
        put(xslot(k) if src is None else src, xslot(k), s_xd, r_x.at[k], device(yh, x, yl, z, 1 - c))

    share_crossed(o, xin.at[yl])
    ls = lax.div(z, 2)
    lt = 2 * lax.rem(z, 2) + c
    for hf in range(2):
        put(lad.at[pl.ds(hf * 256, 256)], lslot(lt, hf), s_l.at[2], r_l.at[lt, hf],
            device(yh, x, yl, z, ls), own=c == ls)

    op = ((1 - yl) * 4 + z) * 2 + c
    arrived(xslot(op), r_x.at[op])
    for d in range(2):
        put(xslot(op), xslot(op), s_xz.at[d], r_x.at[op], device(yh, x, yl, zn[d], c))

    def send_ladder(part):
        for d in range(2):
            hf = d if part == 0 else 1 - d
            put(lad.at[pl.ds(hf * 256, 256)], lslot(lt, hf), s_l.at[d], r_l.at[lt, hf],
                device(yh, x, yl, zn[d], ls))

    send_ladder(0)
    share_crossed(op)

    xsrc = (xn[1], xn[0], lax.rem(x + 2, 4))

    def along_y(i):
        xs_, part = xsrc[i], xt.at[i]
        arrived(part, r_xt.at[i])
        u, core = lax.rem(xs_, 2), lax.div(xs_, 2)
        put(part, mslot(u, q, LP), s_y.at[0, i], r_m.at[u, q, LP], device(yh, x, yh, z, core),
            own=both(edge, c == core))
        put(part, tt.at[i], s_y.at[1, i], r_tt.at[i], device(1 - yh, x, 1 - yl, z, c), cond=edge)
        put(part, mslot(u, q, LP), s_y.at[1, i], r_m.at[u, q, LP], device(1 - yh, x, yh, z, core),
            cond=inner)

    for i in range(2):
        along_y(i)
        put(xt.at[i], xt.at[2], s_tf, r_xt.at[2], device(yh, xn[i], yl, z, c), cond=c == i)

    origin = c == ms

    def spread_amplitudes(k, p):
        arrived(mslot(mu, k, p), r_m.at[mu, k, p], cond=origin)
        for d in range(2):
            put(mslot(mu, k, p), mslot(mu, k, p), s_mx.at[d], r_m.at[mu, k, p],
                device(yh, xn[d], yl, z, c), cond=origin)

    for p in range(LP):
        for e in range(2):
            spread_amplitudes(yh * 2 + e, p)

    def pass_crossed(b):
        k = (b * 4 + lax.rem(z + 3 + 2 * b, 4)) * 2 + c
        arrived(xslot(k), r_x.at[k])
        put(xslot(k), xslot(k), s_xf, r_x.at[k], device(yh, x, yl, lax.rem(z + 1 + 2 * b, 4), c))
        share_crossed(k)

    pass_crossed(yl)
    pass_crossed(1 - yl)
    send_ladder(1)
    for d in range(2):
        k = ((1 - d) * 4 + zn[1 - d]) * 2 + c
        arrived(xslot(k), r_x.at[k])
        share_crossed(k)

    along_y(2)

    kt = (1 - yl) * 2 + c
    for p in range(NP):
        part = tb.at[pl.ds(p * PR, PR)]
        arrived(part, r_t.at[p], cond=edge)
        put(part, mslot(mu, kt, p), s_mt, r_m.at[mu, kt, p], device(yh, x, 1 - yh, z, ms), cond=edge)
        if p < LP:
            for e in range(2):
                spread_amplitudes((1 - yh) * 2 + e, p)

    lane = lax.broadcasted_iota(jnp.int32, (1, 1024), 1)
    slot_a = lax.div(lane, 64)
    slot_b = lax.rem(lane, 64)
    low = lax.broadcasted_iota(jnp.int32, (16, 128), 1) < 64
    low8 = lax.broadcasted_iota(jnp.int32, (8, 128), 1) < 64

    def rest_of_amplitudes(u):
        dist = lax.rem(x - (2 * c + u) + 4, 4)
        for k in range(4):
            done = jnp.logical_or(dist == 0, dist == (1, 3)[k % 2])
            for p in range(LP):
                arrived(mslot(u, k, p), r_m.at[u, k, p], cond=jnp.logical_not(done))
            arrived(mslot(u, k, LP), r_m.at[u, k, LP])

    ldist = [lax.rem(z - (2 * c + u) + 4, 4) for u in range(2)]
    e1 = jnp.where(ldist[0] == 2, 0, 1)
    e0 = 1 - e1

    def rest_of_ladder(e):
        dist = lax.rem(z - (2 * c + e) + 4, 4)
        for hf in range(2):
            for t in range(2):
                arrived(lslot(2 * e + t, hf), r_l.at[2 * e + t, hf],
                        cond=both(dist != (1, 3)[hf], dist != 2))

    def lchunk(t, hf, j):
        return lb.at[rows_of(t * 2 + hf, 256), pl.ds(j * 256, 256)]

    def far_ladder(j):
        for hf in range(2):
            for t in range(2):
                arrived(lchunk(2 * e1 + t, hf, j), r_lf.at[2 * e1 + t, hf, j],
                        cond=lax.rem(z - (2 * c + e1) + 4, 4) == 2)

    def pass_ladder():
        for u in range(2):
            for d in range(2):
                for t in (2 * u, 2 * u + 1):
                    arrived(lslot(t, d), r_l.at[t, d], cond=ldist[u] == (1, 3)[d])
        for j in range(4):
            for u in range(2):
                for d in range(2):
                    for t in (2 * u, 2 * u + 1):
                        put(lchunk(t, d, j), lchunk(t, d, j), s_lf, r_lf.at[t, d, j],
                            device(yh, x, yl, zn[d], c), cond=ldist[u] == (1, 3)[d])

    def apply_mask(u):
        act = jnp.logical_and(slot_a + (32 * c + 16 * u) < cnt[2 * yl], slot_b < cnt[2 * yl + 1])
        mask = jnp.where(act, 1.0, 0.0).astype(BF16)

        @pl.loop(0, 32)
        def _(r):
            mm[u, rows_of(r, 32), :] = mb[u, rows_of(r, 32), :] * mask

    def reorder(u):
        @pl.loop(0, 8)
        def _(ap):
            @pl.loop(0, 16)
            def _(r):
                ff[pl.ds(pl.multiple_of(r * 72, 8), 64), :] = mm[u, rows_of(r, 64), rows_of(ap, 128)].astype(F32)

            for kp in range(32):
                v0 = ff[pl.ds(2 * kp, 16, stride=72), :]
                v1 = ff[pl.ds(2 * kp + 1, 16, stride=72), :]
                turned = pltpu.roll(jnp.where(low, v1, v0), 64, 1)
                pair = jnp.concatenate([jnp.where(low, v0, turned), jnp.where(low, turned, v1)], axis=0)
                rr[rows_of(u * 8 + ap, 32), kp * 128:(kp + 1) * 128] = pair.astype(BF16)

    def ladder_first(u, j):
        @pl.loop(0, 4)
        def _(t):
            rows, cols = rows_of(t, 256), slice(j * 256, (j + 1) * 256)
            pp[rows, cols] = jnp.dot(mm[u, rows, :], lb[rows_of(u, 1024), cols], preferred_element_type=F32)

    def ladder_second(u, j, b, slot):
        rows, cols = rows_of(b, 256), slice(j * 256, (j + 1) * 256)
        part = pp[rows, cols] + jnp.dot(mm[u, rows, :], lb[rows_of(u, 1024), cols], preferred_element_type=F32)
        if slot is None:
            pp[rows, cols] = part
        else:
            cs[slot, :, cols] = part.astype(BF16)

    def crossed(u):
        for n in range(2):
            cols = slice(n * 256, (n + 1) * 256)
            acc[:, cols] = jnp.dot(rr[rows_of(u, 256), :], xb[:, cols], preferred_element_type=F32)

    def back():
        @pl.loop(0, 8)
        def _(ap):
            for jp in range(4):
                cols = slice(jp * 128, (jp + 1) * 128)
                for ih in range(2):
                    v0 = acc[rows_of(ap * 4 + ih, 8), cols]
                    v1 = acc[rows_of(ap * 4 + 2 + ih, 8), cols]
                    turned = pltpu.roll(jnp.where(low8, v1, v0), 64, 1)
                    dd[ap, pl.ds(ih * 64 + 2 * jp, 8, stride=8), :] = jnp.where(low8, v0, turned)
                    dd[ap, pl.ds(ih * 64 + 2 * jp + 1, 8, stride=8), :] = jnp.where(low8, turned, v1)

    own_out = both(edge, origin)

    def give_back(n, u):
        crossed(u)
        back()
        for k in range(4):
            for ap in range(8):
                xs[n, k, :, ap * 128:(ap + 1) * 128] = dd[ap, k * 32:(k + 1) * 32, :].astype(BF16)
            put(xs.at[n, k], xr.at[v], s_o.at[n], r_o.at[v], device(yl, 2 * c + u, k // 2, z, k % 2),
                own=both(own_out, mu == u, q == k))

    u0 = jnp.where(origin, mu, 1 - mu)
    u1 = 1 - u0

    def prepare(u):
        apply_mask(u)
        reorder(u)

    @pl.when(origin)
    def _():
        rest_of_amplitudes(u0)
        prepare(u0)

    for near in (yh, 1 - yh):
        for p in range(LP):
            for u in range(2):
                dist = lax.rem(x - (2 * c + u) + 4, 4)
                for d in range(2):
                    passing = dist == (1, 3)[d]
                    k = near * 2 + d
                    arrived(mslot(u, k, p), r_m.at[u, k, p], cond=passing)
                    put(mslot(u, k, p), mslot(u, k, p), s_mf, r_m.at[u, k, p],
                        device(yh, xn[d], yl, z, c), cond=passing)

    for i in range(3):
        u, core = lax.rem(xsrc[i], 2), lax.div(xsrc[i], 2)
        arrived(tt.at[i], r_tt.at[i], cond=edge)
        put(tt.at[i], mslot(u, kt, LP), s_y.at[2, i], r_m.at[u, kt, LP], device(yh, x, 1 - yh, z, core),
            cond=edge)

    pass_ladder()
    for b in range(2):
        k = (b * 4 + zo) * 2 + c
        arrived(xslot(k), r_x.at[k])
        share_crossed(k)

    @pl.when(jnp.logical_not(origin))
    def _():
        rest_of_amplitudes(u0)
        prepare(u0)

    arrived(xslot(o), r_x.at[o])
    for b in range(2):
        for tz in range(4):
            k = (b * 4 + tz) * 2 + 1 - c
            arrived(xslot(k), r_x.at[k])
    give_back(0, u0)
    rest_of_amplitudes(u1)
    prepare(u1)
    rest_of_ladder(e0)

    def ccol(ref, k, j):
        return ref.at[k, :, pl.ds(j * 256, 256)]

    def to_core(j, k):
        put(ccol(cs, k, j), ccol(cr, k, j), s_c.at[k], r_c.at[k, j], device(yh, x, yl, z, 1 - c))

    def to_chip(j):
        arrived(ccol(cr, 0, j), r_c.at[0, j])
        cols = slice(j * 256, (j + 1) * 256)
        part = pp[rows_of((1 - yl) * 2 + c, 256), cols] + cr[0, :, cols].astype(F32)
        cs[2, :, cols] = part.astype(BF16)
        put(ccol(cs, 2, j), ccol(cr, 2, j), s_c.at[2], r_c.at[2, j], device(yh, x, 1 - yl, z, c))

    def ladder_chunk(j):
        far_ladder(j)
        ladder_second(e1, j, (1 - yl) * 2 + 1 - c, 0)
        to_core(j, 0)
        ladder_second(e1, j, yl * 2 + 1 - c, 1)
        to_core(j, 1)
        ladder_second(e1, j, (1 - yl) * 2 + c, None)
        ladder_second(e1, j, q, None)

    ladder_first(e0, 0)
    ladder_first(e0, 1)
    rest_of_ladder(e1)
    ladder_chunk(0)
    ladder_first(e0, 2)
    to_chip(0)
    ladder_chunk(1)
    ladder_first(e0, 3)
    to_chip(1)
    ladder_chunk(2)
    to_chip(2)
    give_back(1, u1)
    ladder_chunk(3)
    to_chip(3)

    act_out = jnp.logical_and(slot_a + 16 * x < cnt[2 * yh], slot_b < cnt[2 * yh + 1])
    mask_out = jnp.where(act_out, 1.0, 0.0).astype(F32)

    for d in range(3):
        arrived(lad, s_l.at[d], cond=None if d < 2 else c != ls)
    arrived(lb.at[pl.ds(0, 512)], s_lf)
    arrived(amp, s_m.at[0], cond=jnp.logical_not(own_out))
    arrived(amp, s_m.at[1])
    arrived(tb, s_mt, cond=edge)
    for d in range(2):
        arrived(mb.at[0, pl.ds(0, 4 * PR * LP)], s_mx.at[d], cond=origin)
        arrived(xt.at[d], s_t.at[d])
    arrived(mb.at[0, pl.ds(0, 2 * PR * LP)], s_mf)
    arrived(xt.at[2], s_tf)
    for i in range(3):
        arrived(xt.at[i], s_y.at[0, i], cond=jnp.logical_not(both(edge, c == lax.div(xsrc[i], 2))))
        arrived(xt.at[i], s_y.at[1, i])
        arrived(tt.at[i], s_y.at[2, i], cond=edge)
    arrived(xb.at[pl.ds(0, 256)], s_xa)
    arrived(xb.at[pl.ds(0, 2048)], s_xd)
    arrived(xb.at[pl.ds(0, 512)], s_xf)
    for d in range(2):
        arrived(xb.at[pl.ds(0, 512)], s_xz.at[d])
    for j in range(4):
        arrived(ccol(cr, 1, j), r_c.at[1, j])
        arrived(ccol(cr, 2, j), r_c.at[2, j])
    for k in range(3):
        arrived(cs.at[k], s_c.at[k])

    for kk in range(4):
        for k in (2 * kk, 2 * kk + 1):
            arrived(xr.at[k], r_o.at[k])
        got = [xr[k].astype(F32) for k in (2 * kk, 2 * kk + 1)]
        for i in range(4):
            at = i * 64 + kk * 16
            part = jnp.concatenate([g[i * 8:i * 8 + 8] for g in got], axis=0)
            part += cr[1, at:at + 16, :].astype(F32) + cr[2, at:at + 16, :].astype(F32)
            out[at:at + 16, :] = ((pp[rows_of(q * 16 + i * 4 + kk, 16), :] + part) * mask_out).astype(BF16)

    arrived(xs.at[0], s_o.at[0], cond=jnp.logical_not(own_out))
    arrived(xs.at[0, pl.ds(0, 3)], s_o.at[0], cond=own_out)
    arrived(xs.at[1], s_o.at[1])


def per_device(amplitudes, ladder_integrals, crossed_integrals, vir_counts):
    dma = pltpu.SemaphoreType.DMA
    hbm = pl.BlockSpec(memory_space=pl.ANY)
    return pl.pallas_call(
        kernel,
        out_shape=pltpu.VMEM((256, 1024), BF16),
        in_specs=[pl.BlockSpec(memory_space=pltpu.SMEM), hbm, hbm, hbm],
        out_specs=pl.BlockSpec(memory_space=pltpu.VMEM),
        scratch_shapes=[
            pltpu.VMEM((2, 1024, 1024), BF16),
            pltpu.VMEM((2048, 1024), BF16),
            pltpu.VMEM((4096, 512), BF16),
            pltpu.VMEM((256, 1024), BF16),
            pltpu.VMEM((3, 256 // NP, 1024), BF16),
            pltpu.VMEM((3, 256 // NP, 1024), BF16),
            pltpu.VMEM((2, 1024, 1024), BF16),
            pltpu.VMEM((1024, 1024), F32),
            pltpu.VMEM((512, 4096), BF16),
            pltpu.VMEM((1152, 128), F32),
            pltpu.VMEM((256, 512), F32),
            pltpu.VMEM((8, 128, 128), F32),
            pltpu.VMEM((3, 256, 1024), BF16),
            pltpu.VMEM((3, 256, 1024), BF16),
            pltpu.VMEM((2, 4, 32, 1024), BF16),
            pltpu.VMEM((8, 32, 1024), BF16),
            dma((3,)), dma, dma((2,)), dma, dma((2,)), dma, dma((2,)), dma, dma((3, 3)),
            dma, dma, dma((2,)), dma, dma((3,)), dma((2,)),
            dma((2, 4, NP)), dma((NP,)), dma((3,)), dma((3,)), dma((4, 2)), dma((4, 2, 4)), dma((16,)), dma((3, 4)), dma((8,)),
        ],
        compiler_params=pltpu.CompilerParams(
            collective_id=0, has_side_effects=True, vmem_limit_bytes=56 * 1024 * 1024
        ),
        name="residual",
    )(vir_counts, amplitudes, ladder_integrals, crossed_integrals)


def solution(mesh):
    in_specs = (P("occ", "vir"), P("occ", "vir"), P(None, "occ", "vir"), P())
    return jax.shard_map(
        per_device, mesh=mesh, in_specs=in_specs, out_specs=P("occ", "vir"), check_vma=False
    )
```

time: 81.6 us -> 78.3 us (0.960)
  Pallas kernels: 80.7 us -> 77.3 us
    pallas_call x1, Pallas kernels: 80.7 us -> 77.3 us  [per_device(): pl.pallas_call(kernel, out_shape=pltpu.VMEM((256, 1024), BF16), in_specs=...]
where the time goes in v4:
time: 78.3 us; the launch traced here: 78.1 us
  Pallas kernels  77.3 us (99%)
  local copies, waits for them, and re-layouts  0.8 us (1%)
    pallas_call x1, Pallas kernels, per_device(): pl.pallas_call(kernel, out_shape=pltpu.VMEM((256, 1024), BF16), in_specs=...  77.3 us

profile of v4, /device:TPU:1, one launch (start us, length us, event | category | flops | bytes accessed | tf_op | source)
XLA Modules:
  0.0 78.1 jit_solution(10638215621396752770)
XLA Ops:
  0.0 77.3 %residual.1 = bf16[256,1024]{1,0:T(8,128)(2,1)S(1)} custom-call(s32[8]{0:T(128)} %cnt.1, bf16[256,1024]{1,0:T(8,128)(2,1)} %amp.1, bf16[512,1024]{1,0:T(8,128)(2,1)} %lad.1, bf16[2,256,512]{2,1,0:T(8,128)(2,1)} %xin.1), custom_call_target="tpu_custom_call" | custom-call | tf_op jit(solution)/shard_map/residual/pallas_call | solution.py:439
  77.4 0.8 %copy.6 = bf16[256,1024]{1,0:T(8,128)(2,1)} copy(bf16[256,1024]{1,0:T(8,128)(2,1)S(1)} %residual.1) | data formatting | bytes 1048576

commit v5 on v4

--- a/solution.py
+++ b/solution.py
@@ -84,18 +84,17 @@
         return xb.at[rows_of(k, 256)]
 
     barrier = pltpu.get_barrier_semaphore()
-    for dv in range(8):
-        for dq in range(4):
-            if dv == 0 and dq == 0:
-                continue
-            tv = lax.rem(v + dv, 8)
-            tq = lax.rem(q + dq, 4)
-            to = (lax.div(tq, 2) * 4 + z) * 2 + lax.rem(tq, 2)
-            pl.semaphore_signal(barrier, inc=1, device_id=(tv, to), device_id_type=MESH)
-    for tz in zn:
-        for tc in range(2):
-            pl.semaphore_signal(barrier, inc=1, device_id=device(yh, x, yl, tz, tc), device_id_type=MESH)
-    pl.semaphore_wait(barrier, 35)
+    y = yh * 2 + yl
+    peers = [device(yh, x, yl, z, 1 - c)]
+    for tc in range(2):
+        for d in range(2):
+            ty = lax.rem(y + 1 + 2 * d, 4)
+            peers.append(device(yh, xn[d], yl, z, tc))
+            peers.append(device(lax.div(ty, 2), x, lax.rem(ty, 2), z, tc))
+            peers.append(device(yh, x, yl, zn[d], tc))
+    for peer in peers:
+        pl.semaphore_signal(barrier, inc=1, device_id=peer, device_id_type=MESH)
+    pl.semaphore_wait(barrier, len(peers))
 
     put(xin.at[1 - yl], xslot(o), s_xa, r_x.at[o], device(yh, x, 1 - yl, z, c))
     for d in range(2):
@@ -350,6 +349,7 @@
     give_back(0, u0)
     rest_of_amplitudes(u1)
     prepare(u1)
+    give_back(1, u1)
     rest_of_ladder(e0)
 
     def ccol(ref, k, j):
@@ -385,7 +385,6 @@
     to_chip(1)
     ladder_chunk(2)
     to_chip(2)
-    give_back(1, u1)
     ladder_chunk(3)
     to_chip(3)
 

time: 78.3 us -> 77 us (0.983)
  Pallas kernels: 77.3 us -> 76.1 us
    pallas_call x1, Pallas kernels: 77.3 us -> 76.1 us  [per_device(): pl.pallas_call(kernel, out_shape=pltpu.VMEM((256, 1024), BF16), in_specs=...]
where the time goes in v5:
time: 77 us; the launch traced here: 76.9 us
  Pallas kernels  76.1 us (99%)
  local copies, waits for them, and re-layouts  0.8 us (1%)
    pallas_call x1, Pallas kernels, per_device(): pl.pallas_call(kernel, out_shape=pltpu.VMEM((256, 1024), BF16), in_specs=...  76.1 us

profile of v5, /device:TPU:1, one launch (start us, length us, event | category | flops | bytes accessed | tf_op | source)
XLA Modules:
  0.0 76.9 jit_solution(16431193473416576606)
XLA Ops:
  0.0 76.1 %residual.1 = bf16[256,1024]{1,0:T(8,128)(2,1)S(1)} custom-call(s32[8]{0:T(128)} %cnt.1, bf16[256,1024]{1,0:T(8,128)(2,1)} %amp.1, bf16[512,1024]{1,0:T(8,128)(2,1)} %lad.1, bf16[2,256,512]{2,1,0:T(8,128)(2,1)} %xin.1), custom_call_target="tpu_custom_call" | custom-call | tf_op jit(solution)/shard_map/residual/pallas_call | solution.py:438
  76.1 0.8 %copy.6 = bf16[256,1024]{1,0:T(8,128)(2,1)} copy(bf16[256,1024]{1,0:T(8,128)(2,1)S(1)} %residual.1) | data formatting | bytes 1048576
